TPU v7x, 512 devices: a whole 4x4x16 slice. The times are simulated.
512 devices in a mesh: ctx: 128 (over x, z, core), head: 4 (over y).
Axes of the slice: x: 4, y: 4, z: 16, core: 2. Of those that a mesh axis runs over, the one named last changes fastest.
Arguments:
- queries: bfloat16 [4, 16384, 1024], P(None, 'ctx', 'head'), may hold values from -45 to 45
- keys: bfloat16 [4, 16384, 1024], P(None, 'ctx', 'head'), may hold values from -6 to 6
- values: bfloat16 [4, 16384, 1024], P(None, 'ctx', 'head'), may hold values from -6 to 6
- out_weight: bfloat16 [1024, 2048], P(None, 'head'), may hold values from -0.1875 to 0.1875
- global_ids: int32 [4, 2], replicated, may hold values from 0 to 255, as said below
- rand_ids: int32 [4, 256, 4], P(None, 'ctx'), may hold values from 0 to 255, as said below
- rand_count: int32 [4, 256], P(None, 'ctx'), may hold values from 1 to 4
Outputs:
- output: bfloat16 [4, 16384, 2048], P(None, 'ctx', 'head')
Inputs may be any that keep to these rules, and one draw needn't show every extreme that they name: `global_ids`: block ids; the 2 ids of one sequence are distinct. `rand_ids`: block ids of the same sequence. Taking together the 2 query blocks that each of the 4 sequences has on one index of ctx, at most 1 live slots name blocks held by any one index of ctx.
All inputs are finite; a program needn't handle non-finite values.
Results may differ from a plain program's by a relative error of at most 0.0056.
Values may be sent and summed in bfloat16 or wider, within the bound.
A program may use at most 64 MiB of HBM per device.

v0:
```python
import jax
import jax.numpy as jnp
from jax import lax
from jax.sharding import PartitionSpec as P

HEAD_DIM = 128
BLOCK = 64
GLOB = 2
RMAX = 4


def with_halo(cells, sides, width):
    for axis, dim in sides:
        count = lax.axis_size(axis)
        head = lax.slice_in_dim(cells, 0, width, axis=dim)
        tail = lax.slice_in_dim(cells, cells.shape[dim] - width, cells.shape[dim], axis=dim)
        cells = jnp.concatenate(
            [
                lax.ppermute(tail, axis, [(i, (i + 1) % count) for i in range(count)]),
                cells,
                lax.ppermute(head, axis, [((i + 1) % count, i) for i in range(count)]),
            ],
            axis=dim,
        )
    return cells


def slot_table(slot_of, live_flat, slot_total):
    return (
        (slot_of[:, None] == jnp.arange(slot_total, dtype=jnp.int32)[None, :]) & live_flat[:, None]
    ).astype(jnp.int32)


def on_device(queries, keys, values, out_weight, global_ids, rand_ids, rand_count):
    seq_count, seq_rows, local_width = queries.shape
    blocks_here = seq_rows // BLOCK
    heads_here = local_width // HEAD_DIM
    cycle_size = lax.axis_size("ctx")
    my_index = lax.axis_index("ctx")
    request_count = seq_count * blocks_here * RMAX
    capacity = (request_count + cycle_size - 1) // cycle_size
    slot_total = cycle_size * capacity
    key_width = 3 + GLOB + RMAX
    score_scale = HEAD_DIM ** (-0.5)
    token_pairs = jnp.stack([keys, values], 0)
    block_pairs = jnp.stack(
        [
            keys.reshape(seq_count, blocks_here, BLOCK, local_width),
            values.reshape(seq_count, blocks_here, BLOCK, local_width),
        ],
        2,
    ).reshape(seq_count * blocks_here, 2, BLOCK, local_width)
    extended = with_halo(token_pairs, (("ctx", 2),), BLOCK)
    own_blocks = token_pairs.reshape(2, seq_count, blocks_here, BLOCK, local_width)
    shared_owner = global_ids // blocks_here
    shared_local = global_ids % blocks_here
    picker = (
        (shared_local[:, :, None] == jnp.arange(blocks_here, dtype=jnp.int32)[None, None, :])
        & (shared_owner == my_index)[:, :, None]
    ).astype(jnp.bfloat16)
    contribution = jnp.einsum(
        "sgj,xsjtf->xsgtf", picker, own_blocks, preferred_element_type=jnp.float32
    )
    shared_rows = lax.psum(contribution, "ctx").astype(jnp.bfloat16)
    slot_ids = jnp.arange(RMAX, dtype=jnp.int32)
    live_flat = (slot_ids[None, None, :] < rand_count[:, :, None]).reshape(-1)
    owners = (rand_ids // blocks_here).reshape(-1)
    seq_of = jnp.arange(seq_count, dtype=jnp.int32)[:, None, None]
    block_codes = (seq_of * blocks_here + rand_ids % blocks_here).reshape(-1)
    hit_owner = (
        (owners[:, None] == jnp.arange(cycle_size, dtype=jnp.int32)[None, :]) & live_flat[:, None]
    ).astype(jnp.int32)
    rank_within = jnp.sum((jnp.cumsum(hit_owner, axis=0) - hit_owner) * hit_owner, axis=1)
    slot_of = jnp.where(live_flat, owners * capacity + rank_within, 0)
    slot_hits = slot_table(slot_of, live_flat, slot_total)
    requests_out = (jnp.sum(slot_hits * (block_codes[:, None] + 1), axis=0) - 1).reshape(
        cycle_size, capacity
    )
    wanted_here = lax.all_to_all(requests_out, "ctx", split_axis=0, concat_axis=0, tiled=True)
    beside_all = extended.reshape(2, seq_count, blocks_here + 2, BLOCK, local_width)
    window_keys = jnp.stack(
        [beside_all[:, :, offset : offset + blocks_here] for offset in range(3)], 3
    )
    shared_wide = jnp.broadcast_to(
        shared_rows[:, :, None], (2, seq_count, blocks_here, GLOB, BLOCK, local_width)
    )
    local_keys = jnp.concatenate([window_keys, shared_wide], 3)
    query_view = queries.reshape(seq_count, blocks_here, BLOCK, heads_here, HEAD_DIM)
    payload = jnp.take(block_pairs, jnp.maximum(wanted_here, 0).reshape(-1), axis=0).reshape(
        cycle_size, capacity, 2, BLOCK, local_width
    )
    received = lax.all_to_all(payload, "ctx", split_axis=0, concat_axis=0, tiled=True)
    random_rows = jnp.take(received.reshape(slot_total, 2, BLOCK, local_width), slot_of, axis=0)
    random_rows = jnp.moveaxis(
        random_rows.reshape(seq_count, blocks_here, RMAX, 2, BLOCK, local_width), 3, 0
    )
    all_keys = jnp.concatenate([local_keys, random_rows], 3).reshape(
        2, seq_count, blocks_here, key_width * BLOCK, heads_here, HEAD_DIM
    )
    scores = (
        jnp.einsum(
            "sjqhd,sjkhd->sjhqk", query_view, all_keys[0], preferred_element_type=jnp.float32
        )
        * score_scale
    )
    live_slots = jnp.concatenate(
        [
            jnp.ones((seq_count, blocks_here, 3 + GLOB), jnp.bool_),
            slot_ids[None, None, :] < rand_count[:, :, None],
        ],
        2,
    )
    live_cols = jnp.repeat(live_slots, BLOCK, axis=2)[:, :, None, None, :]
    masked = jnp.where(live_cols, scores, -1e30)
    row_peak = jnp.max(masked, axis=-1, keepdims=True)
    weights = jnp.where(live_cols, jnp.exp(masked - row_peak), 0.0)
    row_total = jnp.sum(weights, axis=-1)
    weighted = jnp.einsum(
        "sjhqk,sjkhd->sjqhd",
        weights.astype(jnp.bfloat16),
        all_keys[1],
        preferred_element_type=jnp.float32,
    )
    attention = (
        (weighted / jnp.moveaxis(row_total, 2, 3)[..., None])
        .astype(jnp.bfloat16)
        .reshape(seq_count, seq_rows, local_width)
    )
    projected = jnp.einsum(
        "stf,fo->sto",
        lax.all_gather(attention, "head", axis=2, tiled=True),
        out_weight,
        preferred_element_type=jnp.float32,
    )
    return projected.astype(jnp.bfloat16)


def solution(mesh):
    placed = (
        P(None, "ctx", "head"),
        P(None, "ctx", "head"),
        P(None, "ctx", "head"),
        P(None, "head"),
        P(),
        P(None, "ctx", None),
        P(None, "ctx"),
    )
    return jax.shard_map(
        on_device, mesh=mesh, in_specs=placed, out_specs=P(None, "ctx", "head"), check_vma=False
    )
```

profile of v0, /device:TPU:1, one launch (start us, length us, event | category | flops | bytes accessed | tf_op | source)
XLA Modules:
  0.0 992.5 jit_solution(1690685669492652247)
XLA Ops:
  6.5 0.9 copy.54
  7.6 0.8 and_select_fusion.1
  8.9 0.7 copy.55
  9.7 20.4 %all-to-all-start = ((s32[128,1,1]{2,1,0:T(1,128)}), s32[128,1,1]{2,1,0:T(1,128)S(1)}, u32[]{:S(2)}, u32[]{:S(2)}) async-start(s32[128,1,1]{2,1,0:T(1,128)} %copy.55), calls=%async_computation | async-start | bytes 131072 | tf_op jit(solution)/shard_map/all_to_all | solution.py:79
  30.1 1.1 pad_maximum_fusion.3
  31.2 13.9 %all-to-all-done = s32[128,1,1]{2,1,0:T(1,128)S(1)} async-done(((s32[128,1,1]{2,1,0:T(1,128)}), s32[128,1,1]{2,1,0:T(1,128)S(1)}, u32[]{:S(2)}, u32[]{:S(2)}) %all-to-all-start) | async-done | bytes 544 | tf_op jit(solution)/shard_map/all_to_all | solution.py:79
  45.1 2.4 maximum_reduce_fusion
  47.4 6.3 gather_fusion
  53.7 2.4 compare_reduce_fusion
  56.1 7.4 bitcast_select_fusion
  63.5 7.9 all-to-all-start.1
  71.6 3.5 collective-permute-start
  75.1 1.9 collective-permute-start.1
  78.0 1.8 convolution_bitcast_fusion
  79.8 843.1 %all-reduce.2 = bf16[2,4,2,64,256]{4,2,3,0,1:T(2,128)(2,1)S(1)} all-reduce(f32[2,4,2,64,256]{4,2,3,0,1:T(2,128)} %convolution_bitcast_fusion), channel_id=1, replica_groups=mesh['ctx'=128,'head'=4] {'ctx'}, use_global_device_ids=true, to_apply=%region_0.1 | all-reduce | flops 262144 | bytes 1572864 | tf_op jit(solution)/shard_map/psum | solution.py:64
  923.1 0.8 reshape.190
  924.3 1.1 pad_maximum_fusion
  925.4 0.8 fusion.32
  926.2 0.8 fusion.31
  927.0 0.8 fusion.30
  927.9 1.1 broadcast_dynamic-update-slice_fusion
  929.0 4.1 gather_fusion.1
  933.1 2.3 bitcast_dynamic-update-slice_fusion
  935.4 5.2 fusion.51
  940.6 4.6 squeeze.7
  945.3 5.7 squeeze.6
  951.0 1.9 fusion.6
  952.9 1.2 fusion.52
  954.5 0.6 fusion.24
  955.4 0.9 reshape.191
  956.3 26.6 %all-gather.2.cloned.1.call-done = bf16[4,128,1024]{2,1,0:T(8,128)(2,1)} async-done(((bf16[4,128,256]{2,1,0:T(8,128)(2,1)}), bf16[4,128,1024]{2,1,0:T(8,128)(2,1)}) %all-gather.2.cloned.1.call-update) | async-done | bytes 1048592 | tf_op jit(solution)/shard_map/all_gather | solution.py:131
  982.9 2.7 convolution_convert_fusion
  (49 shorter events, 3.1 us)
Async XLA Ops:
  6.5 976.4 %copy-start = (bf16[1024,512]{1,0:T(8,128)(2,1)S(1)}, bf16[1024,512]{1,0:T(8,128)(2,1)}, u32[]{:S(2)}) copy-start(bf16[1024,512]{1,0:T(8,128)(2,1)} %param.10) | copy-start | bytes 3145732
  9.7 35.4 %all-to-all-start = ((s32[128,1,1]{2,1,0:T(1,128)}), s32[128,1,1]{2,1,0:T(1,128)S(1)}, u32[]{:S(2)}, u32[]{:S(2)}) async-start(s32[128,1,1]{2,1,0:T(1,128)} %copy.55), calls=%async_computation | async-start | bytes 131072 | tf_op jit(solution)/shard_map/all_to_all | solution.py:79
  63.5 8.0 copy-start.1
  63.5 8.0 copy-start.2
  63.5 14.3 %copy-start.5 = (s32[4,2]{0,1:T(2,128)S(1)}, s32[4,2]{0,1:T(2,128)}, u32[]{:S(2)}) copy-start(s32[4,2]{0,1:T(2,128)} %param.11) | copy-start | bytes 100
  63.5 865.5 %all-to-all-start.1 = ((bf16[128,1,2,64,256]{4,3,2,1,0:T(8,128)(2,1)}), bf16[128,1,2,64,256]{4,3,2,1,0:T(8,128)(2,1)}, u32[]{:S(2)}, u32[]{:S(2)}) async-start(bf16[128,1,2,64,256]{4,3,2,1,0:T(8,128)(2,1)} %bitcast_select_fusion), calls=%async_computation.1 | async-start | bytes 16777216 | tf_op jit(solution)/shard_map/all_to_all | solution.py:92
  71.4 911.5 %all-gather.2.cloned.1.call-start = ((), (), s32[]{:S(2)}) async-start(), calls=%async_computation.2 | async-start | bytes 1310720 | tf_op jit(solution)/shard_map/all_gather | solution.py:131
  71.6 852.7 %collective-permute-start = (bf16[2,4,64,256]{3,2,1,0:T(8,128)(2,1)S(1)}, bf16[2,4,64,256]{3,2,1,0:T(8,128)(2,1)}, u32[]{:S(2)}, u32[]{:S(2)}) collective-permute-start(bf16[2,4,64,256]{3,2,1,0:T(8,128)(2,1)S(1)} %get-tuple-element.7), channel_id=1, source_target_pairs={{0,4},{4,8},{8,12},{12,16},{16,20},{20,24},{24,28},{28,32},{32,36}... | collective-permute-start | bytes 786440 | tf_op jit(solution)/shard_map/ppermute | solution.py:19
  75.1 849.2 %collective-permute-start.1 = (bf16[2,4,64,256]{3,2,1,0:T(8,128)(2,1)S(1)}, bf16[2,4,64,256]{3,2,1,0:T(8,128)(2,1)}, u32[]{:S(2)}, u32[]{:S(2)}) collective-permute-start(bf16[2,4,64,256]{3,2,1,0:T(8,128)(2,1)S(1)} %get-tuple-element.8), channel_id=1, source_target_pairs={{4,0},{8,4},{12,8},{16,12},{20,16},{24,20},{28,24},{32,28},{36,32}... | collective-permute-start | bytes 786440 | tf_op jit(solution)/shard_map/ppermute | solution.py:21
  78.0 845.1 %copy-start.4 = (bf16[4,128,256]{2,1,0:T(8,128)(2,1)S(1)}, bf16[4,128,256]{2,1,0:T(8,128)(2,1)}, u32[]{:S(2)}) copy-start(bf16[4,128,256]{2,1,0:T(8,128)(2,1)} %param.7) | copy-start | bytes 786436
  952.9 1.7 copy-start.3
Sparse Core Ops, SparseCore 0:
  956.4 26.4 all-gather.1
where the time goes:
time: 993 us; the launch traced here: 992 us
  blocking collectives  843 us (85%)
  waiting for transfers between devices  40.5 us (4%)
  local copies, waits for them, and re-layouts  35.2 us (4%)
  starting transfers between devices  33.8 us (3%)
  other arithmetic  19.2 us (2%)
  between operations  13.6 us (1%)
    psum x1, blocking collectives, on_device(): shared_rows = lax.psum(contribution, 'ctx').astype(jnp.bfloat16)  843 us
    all_gather x1, waiting for transfers between devices, on_device(): lax.all_gather(attention, 'head', axis=2, tiled=True)  26.6 us
    all_to_all x1, starting transfers between devices, on_device(): lax.all_to_all(requests_out, 'ctx', split_axis=0, concat_axis=0, tiled=True)  20.4 us
  transfers between devices with their start and end apart: 5, of which 2 were waited for; matrix products, arithmetic and copies ran while one was open for 1% of the time, Pallas kernels for 0%

commit v1 on v0

v1 whole, which is shorter than its diff:
```python
import jax
import jax.numpy as jnp
from jax import lax
from jax.experimental import pallas as pl
from jax.experimental.pallas import tpu as pltpu
from jax.sharding import PartitionSpec as P

HEAD_DIM = 128
BLOCK = 64
GLOB = 2
RMAX = 4
NX, NZ, NC = 4, 16, 2
ROW = NX * NC
SEQS = 4
BPD = 2
OWN = SEQS * BPD
CAP = 16
PAIRS = 4
HALF = OWN // 2
MESH = pl.DeviceIdType.MESH


def exchange_kernel(
    kb, vb, req, gcode, gown, rcv, glob, halo_k, halo_v,
    gath0, gath1, gath2, gath3, offer0, offer1, offer2, offer3, pack, cand, pick, req_in, req_s,
    own_sem, z_send, z_recv, x_send, x_recv, c_send, c_recv, g_send, g_recv,
    h_send, h_recv, r_send, r_recv, s_sem, gl_sem,
):
    gath = (gath0, gath1, gath2, gath3)
    cand_in = (offer0, offer1, offer2, offer3)
    ctx = lax.axis_index("ctx")
    head = lax.axis_index("head")
    x, z, c = ctx // (NZ * NC), (ctx // NC) % NZ, ctx % NC
    me = x * NC + c

    def at_z(step):
        return (x * (NZ * NC) + ((z + step + NZ) % NZ) * NC + c, head)

    def at_row(r):
        return ((r // NC) * (NZ * NC) + z * NC + r % NC, head)

    count = NX * NZ * NC
    right = ((ctx + 1) % count, head)
    left = ((ctx + count - 1) % count, head)

    own = [
        pltpu.make_async_copy(
            (kb, vb)[p % 2].at[:, :, pl.ds((p // 2) * HEAD_DIM, HEAD_DIM)],
            gath[p].at[pl.ds(0, OWN)],
            own_sem.at[p],
        )
        for p in range(PAIRS)
    ]
    for copy in own:
        copy.start()
    own_req = pltpu.make_async_copy(req.at[0], req_s.at[0], s_sem.at[0])
    own_req.start()

    barrier = pltpu.get_barrier_semaphore()
    peers = [at_z(1), at_z(-1), right, left] + [at_row((me + k) % ROW) for k in range(1, ROW)]
    for peer in peers:
        pl.semaphore_signal(barrier, inc=1, device_id=peer, device_id_type=MESH)
    pl.semaphore_wait(barrier, len(peers))

    def req_copy(k):
        return pltpu.make_async_remote_copy(
            src_ref=req.at[k], dst_ref=req_in.at[k],
            send_sem=r_send.at[k], recv_sem=r_recv.at[k],
            device_id=at_row((me + ROW - k) % ROW), device_id_type=MESH,
        )

    for k in range(1, ROW):
        req_copy(k).start()

    def z_copy(p, way, t, a):
        if way == 0:
            src, dst, peer = (-t) % NZ, (-t - 1) % NZ, at_z(1)
        else:
            src, dst, peer = t, t + 1, at_z(-1)
        return pltpu.make_async_remote_copy(
            src_ref=gath[p].at[pl.ds(src * OWN + a * HALF, HALF)],
            dst_ref=gath[p].at[pl.ds(dst * OWN + a * HALF, HALF)],
            send_sem=z_send.at[p, (way * 8 + t) * 2 + a],
            recv_sem=z_recv.at[p, (way * 8 + t) * 2 + a],
            device_id=peer, device_id_type=MESH,
        )

    def used(way, t, a):
        return t < 7 or a == way

    def z_first(p):
        for a in range(2):
            for way in range(2):
                z_copy(p, way, 0, a).start()

    for copy in own:
        copy.wait()
    z_first(0)

    halos = []
    for i, (src, dst) in enumerate(((kb, halo_k), (vb, halo_v))):
        for side in range(2):
            halos.append(
                [
                    pltpu.make_async_remote_copy(
                        src_ref=src.at[2 * s + 1 - side], dst_ref=dst.at[side, s],
                        send_sem=h_send.at[(i * 2 + side) * SEQS + s],
                        recv_sem=h_recv.at[(i * 2 + side) * SEQS + s],
                        device_id=(right, left)[side], device_id_type=MESH,
                    )
                    for s in range(SEQS)
                ]
            )
    for group in halos:
        for copy in group:
            copy.start()

    own_req.wait()
    for k in range(1, ROW):
        req_copy(k).wait()
    rest = [
        pltpu.make_async_copy(req_in.at[k], req_s.at[k], s_sem.at[k]) for k in range(1, ROW)
    ]
    for copy in rest:
        copy.start()
    for copy in rest:
        copy.wait()

    def x_copy(p, k):
        return pltpu.make_async_remote_copy(
            src_ref=pack.at[p, k], dst_ref=rcv.at[p, k],
            send_sem=x_send.at[p, k], recv_sem=x_recv.at[p, k],
            device_id=at_row((me + k) % ROW), device_id_type=MESH,
        )

    def c_copy(p, k):
        return pltpu.make_async_remote_copy(
            src_ref=cand.at[p, k], dst_ref=cand_in[p].at[k],
            send_sem=c_send.at[p, k], recv_sem=c_recv.at[p, k],
            device_id=at_row((me + k) % ROW), device_id_type=MESH,
        )

    def g_copy(p, k):
        return pltpu.make_async_remote_copy(
            src_ref=pick.at[p], dst_ref=glob.at[p, k],
            send_sem=g_send.at[p, k], recv_sem=g_recv.at[p, k],
            device_id=at_row((me + k) % ROW), device_id_type=MESH,
        )

    def self_copies(p):
        return (
            pltpu.make_async_copy(pack.at[p, 0], rcv.at[p, 0], x_send.at[p, 0]),
            pltpu.make_async_copy(pick.at[p], glob.at[p, 0], g_send.at[p, 0]),
        )

    def one_pair(p):
        for t in range(1, 8):
            for a in range(2):
                for way in range(2):
                    z_copy(p, way, t - 1, a).wait_recv()
                    if used(way, t, a):
                        z_copy(p, way, t, a).start()
        for way in range(2):
            z_copy(p, way, 7, way).wait_recv()

        if p < PAIRS - 1:
            z_first(p + 1)

        def offer(k, carry):
            cand[p, k] = gath[p][gcode[(me + k) % ROW]]

            @pl.when(k > 0)
            def _():
                c_copy(p, k).start()

            return carry

        lax.fori_loop(0, ROW, offer, 0)
        cand_in[p][0] = cand[p, 0]

        def fill(k, carry):
            for n in range(CAP):
                pack[p, k, n] = gath[p][req_s[k, 0, n]]

            @pl.when(k > 0)
            def _():
                x_copy(p, k).start()

            return carry

        lax.fori_loop(0, ROW, fill, 0)

        def landed(k, carry):
            c_copy(p, k).wait_recv()
            return carry

        lax.fori_loop(1, ROW, landed, 0)
        pick[p] = cand_in[p][gown[0]]

        def spread(k, carry):
            g_copy(p, k).start()
            return carry

        lax.fori_loop(1, ROW, spread, 0)
        for copy in self_copies(p):
            copy.start()

    for p in range(PAIRS):
        one_pair(p)

    for group in halos:
        for copy in group:
            copy.wait()

    def finish(p):
        for way in range(2):
            for t in range(8):
                for a in range(2):
                    if used(way, t, a):
                        z_copy(p, way, t, a).wait_send()
        for copy in self_copies(p):
            copy.wait()

        def ends(k, carry):
            c_copy(p, k).wait_send()
            x_copy(p, k).wait()
            g_copy(p, k).wait()
            return carry

        lax.fori_loop(1, ROW, ends, 0)

    for p in range(PAIRS):
        finish(p)


def exchange(kb, vb, req, gcode, gown):
    width = kb.shape[-1]
    block = (BLOCK, HEAD_DIM)
    dma = pltpu.SemaphoreType.DMA
    bf16 = jnp.bfloat16
    hbm = pl.BlockSpec(memory_space=pl.ANY)
    smem = pl.BlockSpec(memory_space=pltpu.SMEM)
    return pl.pallas_call(
        exchange_kernel,
        out_shape=(
            jax.ShapeDtypeStruct((PAIRS, ROW, CAP) + block, bf16),
            jax.ShapeDtypeStruct((PAIRS, ROW) + block, bf16),
            jax.ShapeDtypeStruct((2, SEQS, BLOCK, width), bf16),
            jax.ShapeDtypeStruct((2, SEQS, BLOCK, width), bf16),
        ),
        in_specs=[hbm, hbm, pl.BlockSpec(memory_space=pltpu.VMEM), smem, smem],
        out_specs=(hbm, hbm, hbm, hbm),
        scratch_shapes=[
            *([pltpu.VMEM((NZ * OWN,) + block, bf16)] * PAIRS),
            *([pltpu.VMEM((ROW,) + block, bf16)] * PAIRS),
            pltpu.VMEM((PAIRS, ROW, CAP) + block, bf16),
            pltpu.VMEM((PAIRS, ROW) + block, bf16),
            pltpu.VMEM((PAIRS,) + block, bf16),
            pltpu.VMEM((ROW, 8, 128), jnp.int32),
            pltpu.SMEM((ROW, 8, 128), jnp.int32),
            dma((PAIRS,)),
            dma((PAIRS, 32)), dma((PAIRS, 32)),
            dma((PAIRS, ROW)), dma((PAIRS, ROW)),
            dma((PAIRS, ROW)), dma((PAIRS, ROW)),
            dma((PAIRS, ROW)), dma((PAIRS, ROW)),
            dma((4 * SEQS,)), dma((4 * SEQS,)),
            dma((ROW,)), dma((ROW,)),
            dma((ROW,)), dma((1,)),
        ],
        compiler_params=pltpu.CompilerParams(
            collective_id=0, has_side_effects=True, vmem_limit_bytes=40 << 20
        ),
        name="exchange",
    )(kb, vb, req, gcode, gown)


def attend_kernel(slots, gslots, counts, q, kb, vb, hk, hv, g0, g1, *rest):
    rand, out = rest[: BPD * RMAX], rest[BPD * RMAX]
    s = pl.program_id(0)
    scale = HEAD_DIM ** (-0.5)
    width = (3 + GLOB + RMAX) * BLOCK
    column = lax.broadcasted_iota(jnp.int32, (BLOCK, width), 1)
    for j in range(BPD):
        live = column < (3 + GLOB) * BLOCK + counts[s * BPD + j] * BLOCK
        for h in range(2):
            lanes = slice(h * HEAD_DIM, (h + 1) * HEAD_DIM)

            def rows(own, halo, p):
                window = [halo[0, 0, :, lanes], own[0, :, lanes], own[1, :, lanes], halo[1, 0, :, lanes]]
                picked = [rand[j * RMAX + r][p, 0] for r in range(RMAX)]
                return jnp.concatenate(window[j : j + 3] + [g0[p, 0], g1[p, 0]] + picked, axis=0)

            keys = rows(kb, hk, 2 * h)
            values = rows(vb, hv, 2 * h + 1)
            scores = lax.dot_general(
                q[j, :, lanes], keys, (((1,), (1,)), ((), ())), preferred_element_type=jnp.float32
            ) * scale
            masked = jnp.where(live, scores, -1e30)
            peak = jnp.max(masked, axis=-1, keepdims=True)
            weights = jnp.where(live, jnp.exp(masked - peak), 0.0)
            total = jnp.sum(weights, axis=-1, keepdims=True)
            weighted = jnp.dot(
                weights.astype(jnp.bfloat16), values, preferred_element_type=jnp.float32
            )
            out[j, :, lanes] = (weighted / total).astype(jnp.bfloat16)


def attend(slots, gslots, counts, q, kb, vb, hk, hv, glob, rcv):
    width = q.shape[-1]
    pair = pl.BlockSpec((BPD, BLOCK, width), lambda s, *_: (s, 0, 0))
    halo = pl.BlockSpec((2, 1, BLOCK, width), lambda s, *_: (0, s, 0, 0))

    def shared(g):
        return pl.BlockSpec(
            (PAIRS, 1, BLOCK, HEAD_DIM), lambda s, sl, gs, ct: (0, gs[s * GLOB + g], 0, 0)
        )

    def random(n):
        return pl.BlockSpec(
            (PAIRS, 1, BLOCK, HEAD_DIM), lambda s, sl, gs, ct: (0, sl[s * BPD * RMAX + n], 0, 0)
        )

    return pl.pallas_call(
        attend_kernel,
        out_shape=jax.ShapeDtypeStruct(q.shape, q.dtype),
        grid_spec=pltpu.PrefetchScalarGridSpec(
            num_scalar_prefetch=3,
            grid=(SEQS,),
            in_specs=[pair, pair, pair, halo, halo, shared(0), shared(1)]
            + [random(n) for n in range(BPD * RMAX)],
            out_specs=pair,
        ),
        name="attend",
    )(slots, gslots, counts, q, kb, vb, hk, hv, glob, glob, *([rcv] * (BPD * RMAX)))


def on_device(queries, keys, values, out_weight, global_ids, rand_ids, rand_count):
    seq_count, seq_rows, width = queries.shape
    q = queries.reshape(OWN, BLOCK, width)
    kb = keys.reshape(OWN, BLOCK, width)
    vb = values.reshape(OWN, BLOCK, width)
    ctx = lax.axis_index("ctx")
    my_z = (ctx // NC) % NZ
    me = (ctx // (NZ * NC)) * NC + ctx % NC

    def place(ids, seq):
        owner = ids // BPD
        row = (owner // (NZ * NC)) * NC + owner % NC
        code = (((owner // NC) % NZ - my_z) % NZ) * OWN + seq * BPD + ids % BPD
        return row, code

    seq_of = jnp.arange(SEQS, dtype=jnp.int32)
    row, code = place(rand_ids, seq_of[:, None, None])
    live = (jnp.arange(RMAX, dtype=jnp.int32) < rand_count[:, :, None]).reshape(-1)
    turn = ((me - row) % ROW).reshape(-1)
    code = code.reshape(-1)
    number = jnp.arange(turn.shape[0], dtype=jnp.int32)
    same = (turn[:, None] == turn[None, :]) & live[None, :] & (number[None, :] < number[:, None])
    rank = jnp.sum(same.astype(jnp.int32), axis=1)
    slots = jnp.where(live, turn * CAP + rank, 0)
    place_of = jnp.arange(ROW, dtype=jnp.int32)[:, None] * CAP + jnp.minimum(
        jnp.arange(128, dtype=jnp.int32), CAP
    )
    valid = jnp.arange(128, dtype=jnp.int32) < CAP
    hit = (place_of[:, :, None] == slots[None, None, :]) & live & valid[None, :, None]
    req = jnp.sum(jnp.where(hit, code[None, None, :], 0), axis=2)
    req = jnp.broadcast_to(req[:, None, :], (ROW, 8, 128))

    grow, gcode = place(global_ids, seq_of[:, None])
    grow, gcode = grow.reshape(-1), gcode.reshape(-1)
    gown = ((me - grow) % ROW)[me].reshape(1)
    gslots = (me - jnp.arange(ROW, dtype=jnp.int32)) % ROW

    rcv, glob, halo_k, halo_v = exchange(kb, vb, req, gcode, gown)
    attention = attend(
        slots, gslots, rand_count.reshape(-1), q, kb, vb, halo_k, halo_v, glob,
        rcv.reshape(PAIRS, ROW * CAP, BLOCK, HEAD_DIM),
    ).reshape(seq_count, seq_rows, width)
    projected = jnp.einsum(
        "stf,fo->sto",
        lax.all_gather(attention, "head", axis=2, tiled=True),
        out_weight,
        preferred_element_type=jnp.float32,
    )
    return projected.astype(jnp.bfloat16)


def solution(mesh):
    placed = (
        P(None, "ctx", "head"),
        P(None, "ctx", "head"),
        P(None, "ctx", "head"),
        P(None, "head"),
        P(),
        P(None, "ctx", None),
        P(None, "ctx"),
    )
    return jax.shard_map(
        on_device, mesh=mesh, in_specs=placed, out_specs=P(None, "ctx", "head"), check_vma=False
    )
```

time: 993 us -> 252 us (0.25)
  blocking collectives: 843 us -> 0 us
  Pallas kernels: 0 us -> 193 us
  starting transfers between devices: 33.8 us -> 0.01 us
  local copies, waits for them, and re-layouts: 35.2 us -> 10 us
  other arithmetic: 19.2 us -> 3.19 us
  waiting for transfers between devices: 40.5 us -> 29.2 us
    psum x1 -> x0, blocking collectives: 843 us -> none  [on_device(): shared_rows = lax.psum(contribution, 'ctx').astype(jnp.bfloat16)]
    pallas_call x0 -> x2, Pallas kernels: none -> 193 us  [the longest x1 185 us: exchange(): pl.pallas_call(exchange_kernel, out_shape=(jax.ShapeDtypeStruct((PAIRS, R...]
    all_to_all x2 -> x0, starting transfers between devices: 28.3 us -> none  [the longest x1 20.4 us: on_device(): lax.all_to_all(requests_out, 'ctx', split_axis=0, concat_axis=0, tiled=True)]
    all_to_all x2 -> x0, waiting for transfers between devices: 13.9 us -> none  [the longest x1 13.9 us: on_device(): lax.all_to_all(requests_out, 'ctx', split_axis=0, concat_axis=0, tiled=True)]
    gather x2 -> x0, local copies, waits for them, and re-layouts: 10.4 us -> none  [the longest x1 6.29 us: on_device(): jnp.take(block_pairs, jnp.maximum(wanted_here, 0).reshape(-1), axis=0)]
    squeeze x2 -> x0, local copies, waits for them, and re-layouts: 10.3 us -> none  [the longest x1 5.71 us: on_device(): all_keys[1]]
  transfers between devices with their start and end apart: 5 -> 1, of which waited for: 2 -> 1; matrix products, arithmetic and copies ran while one was open for 1% -> 0% of each run, Pallas kernels for 0% -> 0%
where the time goes in v1:
time: 252 us
  Pallas kernels  193 us (77%)
  waiting for transfers between devices  29.2 us (12%)
  between operations  13.5 us (5%)
  local copies, waits for them, and re-layouts  10 us (4%)
  other arithmetic  3.19 us (1%)
  matrix products  2.73 us (1%)
    pallas_call x1, Pallas kernels, exchange(): pl.pallas_call(exchange_kernel, out_shape=(jax.ShapeDtypeStruct((PAIRS, R...  185 us
    all_gather x1, waiting for transfers between devices, on_device(): lax.all_gather(attention, 'head', axis=2, tiled=True)  29.2 us
    pallas_call x1, Pallas kernels, attend(): pl.pallas_call(attend_kernel, out_shape=jax.ShapeDtypeStruct(q.shape, q.d...  8.33 us
    unnamed x17, local copies, waits for them, and re-layouts  8.13 us
  transfers between devices with their start and end apart: 1, of which 1 were waited for; matrix products, arithmetic and copies ran while one was open for 0% of the time, Pallas kernels for 0%

profile of v1, /device:TPU:1, one launch (start us, length us, event | category | flops | bytes accessed | tf_op | source)
XLA Modules:
  0.0 251.7 jit_solution(9086207004833840712)
XLA Ops:
  6.5 0.0 copy-start
  6.5 0.0 all-gather.2.cloned.1.call-start
  6.5 0.5 and_select_fusion.16.gslots
  7.1 0.8 copy.16
  7.8 0.7 reshape.128.counts
  8.5 0.1 iota_compare_fusion.1
  8.6 0.1 lt.114
  8.7 0.7 fusion.17
  9.4 0.1 copy.19
  9.5 0.1 sub.82
  9.6 0.7 fusion.13
  10.3 0.1 copy.18
  10.4 0.1 reshape.132.gcode
  10.5 0.8 fusion.6
  11.2 0.1 broadcast_in_dim.21
  11.4 0.1 reshape.127
  11.4 0.2 convert_reduce_fusion
  11.7 0.6 dynamic_slice.3.gown
  12.2 0.1 broadcast_add_fusion
  12.3 0.1 select_reduce_fusion
  12.4 0.0 copy-start.3
  12.5 0.9 copy-done.3
  13.4 0.9 copy-done.4
  14.3 184.7 %exchange.1 = (bf16[4,8,16,64,128]{4,3,2,1,0:T(8,128)(2,1)S(1)}, bf16[4,8,64,128]{3,2,1,0:T(8,128)(2,1)S(1)}, bf16[2,4,64,256]{3,2,1,0:T(8,128)(2,1)S(1)}, bf16[2,4,64,256]{3,2,1,0:T(8,128)(2,1)S(1)}) custom-call(bf16[8,64,256]{2,1,0:T(8,128)(2,1)S(1)} %bitcast.18, bf16[8,64,256]{2,1,0:T(8,128)(2,1)S(1)} %bitcast.20, s32[8,8,128]{2,1,0:T(8,128)S(1)} %broadcast_in_dim.24.req, ...), custom_call_target="tpu_custom_call" | custom-call | tf_op jit(solution)/shard_map/exchange/pallas_call | solution.py:243
  199.1 3.2 %copy-done.1 = bf16[4,8,16,64,128]{4,3,2,1,0:T(8,128)(2,1)} copy-done((bf16[4,8,16,64,128]{4,3,2,1,0:T(8,128)(2,1)}, bf16[4,8,16,64,128]{4,3,2,1,0:T(8,128)(2,1)S(1)}, u32[]{:S(2)}) %copy-start.1) | copy-done | bytes 8388632
  202.3 0.8 copy-done.2
  203.1 0.7 copy-done.5
  203.8 0.7 copy-done.6
  204.6 8.3 %attend.1 = bf16[8,64,256]{2,1,0:T(8,128)(2,1)} custom-call(s32[32]{0:T(128)} %copy-done.7, s32[8]{0:T(128)} %and_select_fusion.16.gslots, s32[8]{0:T(128)} %reshape.128.counts, bf16[8,64,256]{2,1,0:T(8,128)(2,1)} %bitcast.22, bf16[8,64,256]{2,1,0:T(8,128)(2,1)} %bitcast.17, bf16[8,64,256]{2,1,0:T(8,128)(2,1)} %bitcast.19, ...), custom_call_target="tpu_custom_call" | custom-call | tf_op jit(solution)/shard_map/attend/pallas_call | solution.py:323
  212.9 0.0 all-gather.2.cloned.1.call-update
  212.9 29.2 %all-gather.2.cloned.1.call-done = bf16[4,128,1024]{2,1,0:T(8,128)(2,1)} async-done(((bf16[4,128,256]{2,1,0:T(8,128)(2,1)}), bf16[4,128,1024]{2,1,0:T(8,128)(2,1)}) %all-gather.2.cloned.1.call-update) | async-done | bytes 1048592 | tf_op jit(solution)/shard_map/all_gather | solution.py:381
  242.1 2.7 %convolution_convert_fusion = bf16[4,128,512]{2,1,0:T(8,128)(2,1)} fusion(bf16[4,128,1024]{2,1,0:T(8,128)(2,1)} %all-gather.2.cloned.1.call-done, bf16[1024,512]{1,0:T(8,128)(2,1)S(1)} %copy-done), kind=kOutput, calls=%fused_computation | convolution fusion | flops 537133056 | bytes 2621440 | tf_op jit(solution)/shard_map/stf,fo->sto/dot_general | solution.py:379
  (16 shorter events, 0.1 us)
Async XLA Ops:
  6.5 235.6 %copy-start = (bf16[1024,512]{1,0:T(8,128)(2,1)S(1)}, bf16[1024,512]{1,0:T(8,128)(2,1)}, u32[]{:S(2)}) copy-start(bf16[1024,512]{1,0:T(8,128)(2,1)} %param.10) | copy-start | bytes 3145732
  6.5 235.6 %all-gather.2.cloned.1.call-start = ((), (), s32[]{:S(2)}) async-start(), calls=%async_computation | async-start | bytes 1310720 | tf_op jit(solution)/shard_map/all_gather | solution.py:381
  11.6 192.9 %copy-start.7 = (s32[32]{0:T(128)}, s32[32]{0:T(128)S(1)}, u32[]{:S(2)}) copy-start(s32[32]{0:T(128)S(1)} %add_select_fusion.slots) | copy-start | bytes 388
  12.4 1.0 copy-start.3
  13.4 0.9 copy-start.4
  199.1 3.2 %copy-start.1 = (bf16[4,8,16,64,128]{4,3,2,1,0:T(8,128)(2,1)}, bf16[4,8,16,64,128]{4,3,2,1,0:T(8,128)(2,1)S(1)}, u32[]{:S(2)}) copy-start(bf16[4,8,16,64,128]{4,3,2,1,0:T(8,128)(2,1)S(1)} %get-tuple-element.12) | copy-start | bytes 25165828
  202.3 0.8 copy-start.2
  203.1 0.7 copy-start.5
  203.8 0.7 copy-start.6
Sparse Core Ops, SparseCore 0:
  213.0 29.0 all-gather.1

commit v2 on v1

v2 whole, which is shorter than its diff:
```python
import jax
import jax.numpy as jnp
from jax import lax
from jax.experimental import pallas as pl
from jax.experimental.pallas import tpu as pltpu
from jax.sharding import PartitionSpec as P

HEAD_DIM = 128
BLOCK = 64
GLOB = 2
RMAX = 4
NX, NZ, NC = 4, 16, 2
ROW = NX * NC
SEQS = 4
BPD = 2
OWN = SEQS * BPD
CAP = 16
PAIRS = 4
SPLIT = 4
PART = OWN // SPLIT
MESH = pl.DeviceIdType.MESH


GROUPS = ((0, 5), (5, 9), (9, 13), (13, 16))
NY = 4


def slot_of(d):
    return 0 if d == 0 else (2 * d - 1 if d < 8 else (15 if d == 8 else 2 * (NZ - d)))


ORDER = sorted(range(NZ), key=slot_of)


def exchange_kernel(
    kb, vb, req, gdist, gsel, gown, rcv, glob, halo_k, halo_v, *scratch
):
    gath = [scratch[p * NZ : (p + 1) * NZ] for p in range(PAIRS)]
    cand_in = scratch[PAIRS * NZ : PAIRS * (NZ + 1)]
    (
        pack, cand, pick, req_in, req_s,
        own_sem, z_send, z_recv, x_send, x_recv, c_send, c_recv, g_send, g_recv,
        h_send, h_recv, r_send, r_recv, s_sem,
    ) = scratch[PAIRS * (NZ + 1) :]
    ctx = lax.axis_index("ctx")
    head = lax.axis_index("head")
    x, z, c = ctx // (NZ * NC), (ctx // NC) % NZ, ctx % NC
    me = x * NC + c

    def at_z(step):
        return (x * (NZ * NC) + ((z + step + NZ) % NZ) * NC + c, head)

    def at_row(r):
        return ((r // NC) * (NZ * NC) + z * NC + r % NC, head)

    count = NX * NZ * NC
    right = ((ctx + 1) % count, head)
    left = ((ctx + count - 1) % count, head)

    own = [
        pltpu.make_async_copy(
            (kb, vb)[p % 2].at[:, :, pl.ds((p // 2) * HEAD_DIM, HEAD_DIM)],
            gath[p][0],
            own_sem.at[p],
        )
        for p in range(PAIRS)
    ]
    for copy in own:
        copy.start()
    own_req = pltpu.make_async_copy(req.at[0], req_s.at[0], s_sem.at[0])
    own_req.start()

    barrier = pltpu.get_barrier_semaphore()
    peers = [at_z(1), at_z(-1), right, left] + [at_row((me + k) % ROW) for k in range(1, ROW)]
    for peer in peers:
        pl.semaphore_signal(barrier, inc=1, device_id=peer, device_id_type=MESH)
    pl.semaphore_wait(barrier, len(peers))

    def req_copy(k):
        return pltpu.make_async_remote_copy(
            src_ref=req.at[k], dst_ref=req_in.at[k],
            send_sem=r_send.at[k], recv_sem=r_recv.at[k],
            device_id=at_row((me + ROW - k) % ROW), device_id_type=MESH,
        )

    for k in range(1, ROW):
        req_copy(k).start()

    def z_copy(p, way, t, a):
        if way == 0:
            src, dst, peer = (-t) % NZ, (-t - 1) % NZ, at_z(1)
        else:
            src, dst, peer = t, t + 1, at_z(-1)
        part = pl.ds(a * PART, PART)
        return pltpu.make_async_remote_copy(
            src_ref=gath[p][src].at[part],
            dst_ref=gath[p][dst].at[part],
            send_sem=z_send.at[p, (way * 8 + t) * SPLIT + a],
            recv_sem=z_recv.at[p, (way * 8 + t) * SPLIT + a],
            device_id=peer, device_id_type=MESH,
        )

    def used(way, t, a):
        return t < 7 or a // (SPLIT // 2) == way

    for copy in own:
        copy.wait()
    for a in range(SPLIT):
        for way in range(2):
            z_copy(0, way, 0, a).start()

    halos = []
    for i, (src, dst) in enumerate(((kb, halo_k), (vb, halo_v))):
        for side in range(2):
            for s in range(SEQS):
                halos.append(
                    pltpu.make_async_remote_copy(
                        src_ref=src.at[2 * s + 1 - side], dst_ref=dst.at[side, s],
                        send_sem=h_send.at[(i * 2 + side) * SEQS + s],
                        recv_sem=h_recv.at[(i * 2 + side) * SEQS + s],
                        device_id=(right, left)[side], device_id_type=MESH,
                    )
                )
    for copy in halos:
        copy.start()

    own_req.wait()
    for k in range(1, ROW):
        req_copy(k).wait()
    rest = [
        pltpu.make_async_copy(req_in.at[k], req_s.at[k], s_sem.at[k]) for k in range(1, ROW)
    ]
    for copy in rest:
        copy.start()
    for copy in rest:
        copy.wait()

    def x_copy(p, g, k):
        low, high = GROUPS[g]
        return pltpu.make_async_remote_copy(
            src_ref=pack.at[p, k, pl.ds(low, high - low)],
            dst_ref=rcv.at[p, k, pl.ds(low, high - low)],
            send_sem=x_send.at[p * len(GROUPS) + g, k],
            recv_sem=x_recv.at[p * len(GROUPS) + g, k],
            device_id=at_row((me + k) % ROW), device_id_type=MESH,
        )

    def c_copy(p, k):
        return pltpu.make_async_remote_copy(
            src_ref=cand.at[p, (me + k) % ROW], dst_ref=cand_in[p].at[k],
            send_sem=c_send.at[p, k], recv_sem=c_recv.at[p, k],
            device_id=at_row((me + k) % ROW), device_id_type=MESH,
        )

    def g_copy(p, k):
        return pltpu.make_async_remote_copy(
            src_ref=pick.at[p], dst_ref=glob.at[p, k],
            send_sem=g_send.at[p, k], recv_sem=g_recv.at[p, k],
            device_id=at_row((me + k) % ROW), device_id_type=MESH,
        )

    def push(p, g):
        low, high = GROUPS[g]
        for n in range(low, high):
            rcv[p, 0, n] = gath[p][ORDER[n]][req_s[0, 0, n]]

        def fill(k, carry):
            for n in range(low, high):
                pack[p, k, n] = gath[p][ORDER[n]][req_s[k, 0, n]]
            x_copy(p, g, k).start()
            return carry

        lax.fori_loop(1, ROW, fill, 0)

    def consider(p, dists):
        def one(q, carry):
            best = cand[p, q]
            for d in dists:
                best = lax.select(gdist[q] == d, gath[p][d][gsel[q]], best)
            cand[p, q] = best
            return carry

        lax.fori_loop(0, ROW, one, 0)

    def spread(p):
        def landed(k, carry):
            c_copy(p, k).wait_recv()
            return carry

        lax.fori_loop(1, ROW, landed, 0)
        chosen = cand_in[p][gown[0]]
        pick[p] = chosen
        glob[p, 0] = chosen

        def send(k, carry):
            g_copy(p, k).start()
            return carry

        lax.fori_loop(1, ROW, send, 0)

    def one_pair(p):
        def first(q, carry):
            cand[p, q] = gath[p][0][gsel[q]]
            return carry

        lax.fori_loop(0, ROW, first, 0)
        for t in range(1, 8):
            for a in range(SPLIT):
                for way in range(2):
                    z_copy(p, way, t - 1, a).wait_recv()
                    if used(way, t, a):
                        z_copy(p, way, t, a).start()
                    if t == 7 and p < PAIRS - 1:
                        z_copy(p + 1, way, 0, a).start()
            consider(p, (t, NZ - t))
            if t % 2 == 0:
                push(p, t // 2 - 1)
            if t == 3 and p > 0:
                spread(p - 1)
        for a in range(SPLIT):
            z_copy(p, a // (SPLIT // 2), 7, a).wait_recv()
        consider(p, (8,))

        def offer(k, carry):
            c_copy(p, k).start()
            return carry

        lax.fori_loop(1, ROW, offer, 0)
        push(p, 3)
        cand_in[p][0] = cand[p, me]

    for p in range(PAIRS):
        one_pair(p)
    spread(PAIRS - 1)

    for copy in halos:
        copy.wait()
    for p in range(PAIRS):
        for way in range(2):
            for t in range(8):
                for a in range(SPLIT):
                    if used(way, t, a):
                        z_copy(p, way, t, a).wait_send()

        def ends(k, carry, p=p):
            c_copy(p, k).wait_send()
            g_copy(p, k).wait()
            for g in range(len(GROUPS)):
                x_copy(p, g, k).wait()
            return carry

        lax.fori_loop(1, ROW, ends, 0)


def exchange(kb, vb, req, gdist, gsel, gown):
    width = kb.shape[-1]
    block = (BLOCK, HEAD_DIM)
    dma = pltpu.SemaphoreType.DMA
    bf16 = jnp.bfloat16
    hbm = pl.BlockSpec(memory_space=pl.ANY)
    vmem = pl.BlockSpec(memory_space=pltpu.VMEM)
    smem = pl.BlockSpec(memory_space=pltpu.SMEM)
    return pl.pallas_call(
        exchange_kernel,
        out_shape=(
            jax.ShapeDtypeStruct((PAIRS, ROW, CAP) + block, bf16),
            jax.ShapeDtypeStruct((PAIRS, ROW) + block, bf16),
            jax.ShapeDtypeStruct((2, SEQS, BLOCK, width), bf16),
            jax.ShapeDtypeStruct((2, SEQS, BLOCK, width), bf16),
        ),
        in_specs=[hbm, hbm, vmem, smem, smem, smem],
        out_specs=(vmem, vmem, vmem, vmem),
        scratch_shapes=[
            *([pltpu.VMEM((OWN,) + block, bf16)] * (PAIRS * NZ)),
            *([pltpu.VMEM((ROW,) + block, bf16)] * PAIRS),
            pltpu.VMEM((PAIRS, ROW, CAP) + block, bf16),
            pltpu.VMEM((PAIRS, ROW) + block, bf16),
            pltpu.VMEM((PAIRS,) + block, bf16),
            pltpu.VMEM((ROW, 8, 128), jnp.int32),
            pltpu.SMEM((ROW, 8, 128), jnp.int32),
            dma((PAIRS,)),
            dma((PAIRS, 16 * SPLIT)), dma((PAIRS, 16 * SPLIT)),
            dma((PAIRS * len(GROUPS), ROW)), dma((PAIRS * len(GROUPS), ROW)),
            dma((PAIRS, ROW)), dma((PAIRS, ROW)),
            dma((PAIRS, ROW)), dma((PAIRS, ROW)),
            dma((4 * SEQS,)), dma((4 * SEQS,)),
            dma((ROW,)), dma((ROW,)),
            dma((ROW,)),
        ],
        compiler_params=pltpu.CompilerParams(
            collective_id=0, has_side_effects=True, vmem_limit_bytes=44 << 20
        ),
        name="exchange",
    )(kb, vb, req, gdist, gsel, gown)


def attend_kernel(slots, gslots, counts, q, kb, vb, hk, hv, glob, rcv, w, out, att, att_in, send, recv):
    ctx = lax.axis_index("ctx")
    y = lax.axis_index("head")
    barrier = pltpu.get_barrier_semaphore()
    for k in range(1, NY):
        pl.semaphore_signal(
            barrier, inc=1, device_id=(ctx, (y + k) % NY), device_id_type=MESH
        )

    scale = HEAD_DIM ** (-0.5)
    width = (3 + GLOB + RMAX) * BLOCK
    column = lax.broadcasted_iota(jnp.int32, (BLOCK, width), 1)

    def y_copy(k, h):
        lanes = pl.ds(h * HEAD_DIM, HEAD_DIM)
        return pltpu.make_async_remote_copy(
            src_ref=att.at[:, lanes], dst_ref=att_in.at[k - 1, :, lanes],
            send_sem=send.at[k, h], recv_sem=recv.at[k, h],
            device_id=(ctx, (y + k) % NY), device_id_type=MESH,
        )

    for h in range(2):
        lanes = slice(h * HEAD_DIM, (h + 1) * HEAD_DIM)

        def one_seq(s, carry, h=h, lanes=lanes):
            def rows(own, halo, p, j):
                window = [
                    halo[0, s, :, lanes], own[2 * s, :, lanes],
                    own[2 * s + 1, :, lanes], halo[1, s, :, lanes],
                ]
                shared = [glob[p, gslots[s * GLOB + g]] for g in range(GLOB)]
                picked = [rcv[p, slots[(s * BPD + j) * RMAX + r]] for r in range(RMAX)]
                return jnp.concatenate(window[j : j + 3] + shared + picked, axis=0)

            for j in range(BPD):
                live = column < (3 + GLOB) * BLOCK + counts[s * BPD + j] * BLOCK
                scores = lax.dot_general(
                    q[2 * s + j, :, lanes], rows(kb, hk, 2 * h, j), (((1,), (1,)), ((), ())),
                    preferred_element_type=jnp.float32,
                ) * scale
                masked = jnp.where(live, scores, -1e30)
                peak = jnp.max(masked, axis=-1, keepdims=True)
                weights = jnp.where(live, jnp.exp(masked - peak), 0.0)
                total = jnp.sum(weights, axis=-1, keepdims=True)
                weighted = jnp.dot(
                    weights.astype(jnp.bfloat16), rows(vb, hv, 2 * h + 1, j),
                    preferred_element_type=jnp.float32,
                )
                at = pl.ds(pl.multiple_of((2 * s + j) * BLOCK, BLOCK), BLOCK)
                att[at, lanes] = (weighted / total).astype(jnp.bfloat16)
            return carry

        lax.fori_loop(0, SEQS, one_seq, 0)
        if h == 0:
            pl.semaphore_wait(barrier, NY - 1)
        for k in range(1, NY):
            y_copy(k, h).start()

    def rows_of(k):
        return w[pl.ds(pl.multiple_of(((y + NY - k) % NY) * 256, 256), 256), :]

    for k in range(1, NY):
        for h in range(2):
            y_copy(k, h).wait_recv()

    def project(i, carry):
        at = pl.ds(pl.multiple_of(i * 128, 128), 128)
        total = jnp.dot(att[at, :], rows_of(0), preferred_element_type=jnp.float32)
        for k in range(1, NY):
            total += jnp.dot(att_in[k - 1, at, :], rows_of(k), preferred_element_type=jnp.float32)
        out[at, :] = total.astype(jnp.bfloat16)
        return carry

    lax.fori_loop(0, 4, project, 0)
    for k in range(1, NY):
        for h in range(2):
            y_copy(k, h).wait_send()


def attend(slots, gslots, counts, q, kb, vb, hk, hv, glob, rcv, w):
    rows = OWN * BLOCK
    width = q.shape[-1]
    vmem = pl.BlockSpec(memory_space=pltpu.VMEM)
    smem = pl.BlockSpec(memory_space=pltpu.SMEM)
    dma = pltpu.SemaphoreType.DMA
    return pl.pallas_call(
        attend_kernel,
        out_shape=jax.ShapeDtypeStruct((rows, w.shape[1]), q.dtype),
        in_specs=[smem] * 3 + [vmem] * 8,
        out_specs=vmem,
        scratch_shapes=[
            pltpu.VMEM((rows, width), jnp.bfloat16),
            pltpu.VMEM((NY - 1, rows, width), jnp.bfloat16),
            dma((NY, 2)), dma((NY, 2)),
        ],
        compiler_params=pltpu.CompilerParams(
            collective_id=1, has_side_effects=True, vmem_limit_bytes=30 << 20
        ),
        name="attend",
    )(slots, gslots, counts, q, kb, vb, hk, hv, glob, rcv, w)


def on_device(queries, keys, values, out_weight, global_ids, rand_ids, rand_count):
    seq_count, seq_rows, width = queries.shape
    q = queries.reshape(OWN, BLOCK, width)
    kb = keys.reshape(OWN, BLOCK, width)
    vb = values.reshape(OWN, BLOCK, width)
    ctx = lax.axis_index("ctx")
    my_z = (ctx // NC) % NZ
    me = (ctx // (NZ * NC)) * NC + ctx % NC

    def place(ids, seq):
        owner = ids // BPD
        row = (owner // (NZ * NC)) * NC + owner % NC
        dist = ((owner // NC) % NZ - my_z) % NZ
        return row, dist, seq * BPD + ids % BPD

    seq_of = jnp.arange(SEQS, dtype=jnp.int32)
    row, dist, choice = place(rand_ids, seq_of[:, None, None])
    live = (jnp.arange(RMAX, dtype=jnp.int32) < rand_count[:, :, None]).reshape(-1)
    where = jnp.where(dist < 8, jnp.maximum(2 * dist - 1, 0), 2 * (NZ - dist))
    where = jnp.where(dist == 8, CAP - 1, where)
    slots = jnp.where(live, (((me - row) % ROW) * CAP + where).reshape(-1), 0)
    lane = jnp.arange(128, dtype=jnp.int32)
    place_of = jnp.arange(ROW, dtype=jnp.int32)[:, None] * CAP + lane
    hit = (place_of[:, :, None] == slots) & live & (lane < CAP)[None, :, None]
    req = jnp.max(jnp.where(hit, choice.reshape(-1), 0), axis=2)
    req = jnp.broadcast_to(req[:, None, :], (ROW, 8, 128))

    grow, gdist, gsel = place(global_ids, seq_of[:, None])
    gown = ((me - grow.reshape(-1)) % ROW)[me].reshape(1)
    gslots = (me - jnp.arange(ROW, dtype=jnp.int32)) % ROW

    rcv, glob, halo_k, halo_v = exchange(kb, vb, req, gdist.reshape(-1), gsel.reshape(-1), gown)
    return attend(
        slots, gslots, rand_count.reshape(-1), q, kb, vb, halo_k, halo_v, glob,
        rcv.reshape(PAIRS, ROW * CAP, BLOCK, HEAD_DIM), out_weight,
    ).reshape(seq_count, seq_rows, out_weight.shape[1])


def solution(mesh):
    placed = (
        P(None, "ctx", "head"),
        P(None, "ctx", "head"),
        P(None, "ctx", "head"),
        P(None, "head"),
        P(),
        P(None, "ctx", None),
        P(None, "ctx"),
    )
    return jax.shard_map(
        on_device, mesh=mesh, in_specs=placed, out_specs=P(None, "ctx", "head"), check_vma=False
    )
```

time: 252 us -> 173 us (0.69)
  waiting for transfers between devices: 29.2 us -> 0 us
  Pallas kernels: 193 us -> 164 us
  between operations: 13.5 us -> 0.08 us
  local copies, waits for them, and re-layouts: 10 us -> 7.1 us
  matrix products: 2.73 us -> 0 us
    pallas_call x1, Pallas kernels: 185 us -> 143 us  [exchange(): pl.pallas_call(exchange_kernel, out_shape=(jax.ShapeDtypeStruct((PAIRS, R...]
    all_gather x1 -> x0, waiting for transfers between devices: 29.2 us -> none  [on_device(): lax.all_gather(attention, 'head', axis=2, tiled=True)]
    pallas_call x1, Pallas kernels: 8.33 us -> 20.4 us  [attend(): pl.pallas_call(attend_kernel, out_shape=jax.ShapeDtypeStruct((rows, w.sha...]
    dot_general x1 -> x0, matrix products: 2.73 us -> none  [on_device(): jnp.einsum('stf,fo->sto', lax.all_gather(attention, 'head', axis=2, tiled...]
    unnamed x17 -> x10, local copies, waits for them, and re-layouts: 8.13 us -> 5.63 us
  transfers between devices with their start and end apart: 1 -> 0, of which waited for: 1 -> 0; matrix products, arithmetic and copies ran while one was open for 0% -> 0% of each run, Pallas kernels for 0% -> 0%
where the time goes in v2:
time: 173 us
  Pallas kernels  164 us (95%)
  local copies, waits for them, and re-layouts  7.1 us (4%)
  other arithmetic  1.8 us (1%)
    pallas_call x1, Pallas kernels, exchange(): pl.pallas_call(exchange_kernel, out_shape=(jax.ShapeDtypeStruct((PAIRS, R...  143 us
    pallas_call x1, Pallas kernels, attend(): pl.pallas_call(attend_kernel, out_shape=jax.ShapeDtypeStruct((rows, w.sha...  20.4 us
    unnamed x10, local copies, waits for them, and re-layouts  5.63 us

profile of v2, /device:TPU:1, one launch (start us, length us, event | category | flops | bytes accessed | tf_op | source)
XLA Modules:
  0.0 172.7 jit_solution(15661302318712676472)
XLA Ops:
  0.0 0.8 copy.18
  0.8 0.1 reshape.103.counts
  0.9 0.1 iota_compare_fusion
  1.0 0.1 lt.103
  1.1 0.7 fusion.13
  1.8 0.1 copy.22
  1.9 0.1 sub.91
  2.0 0.6 dynamic_slice.3.gown
  2.6 0.1 copy.20
  2.7 0.1 reshape.108.gdist
  2.7 0.1 copy.21
  2.8 0.1 reshape.109.gsel
  2.9 0.1 iota_add_fusion
  3.0 0.8 fusion.4
  3.8 0.1 reshape.107
  3.8 0.1 reshape.102
  3.9 0.1 select_reduce_fusion
  4.1 0.0 copy-start.1
  4.1 0.9 copy-done.1
  5.0 0.0 copy-start.2
  5.0 0.9 copy-done.2
  6.0 143.3 %exchange.1 = (bf16[4,8,16,64,128]{4,3,2,1,0:T(8,128)(2,1)S(1)}, bf16[4,8,64,128]{3,2,1,0:T(8,128)(2,1)S(1)}, bf16[2,4,64,256]{3,2,1,0:T(8,128)(2,1)S(1)}, bf16[2,4,64,256]{3,2,1,0:T(8,128)(2,1)S(1)}) custom-call(bf16[8,64,256]{2,1,0:T(8,128)(2,1)S(1)} %bitcast.7, bf16[8,64,256]{2,1,0:T(8,128)(2,1)S(1)} %bitcast.9, s32[8,8,128]{2,1,0:T(8,128)S(1)} %broadcast_in_dim.19.req, ...), custom_call_target="tpu_custom_call" | custom-call | tf_op jit(solution)/shard_map/exchange/pallas_call | solution.py:263
  149.3 0.0 copy-start
  149.3 1.2 copy-done
  150.5 0.0 copy-start.3
  150.5 0.9 copy-done.3
  151.5 20.4 %attend.1 = bf16[512,512]{1,0:T(8,128)(2,1)S(1)} custom-call(s32[32]{0:T(128)S(1)} %broadcast_select_fusion.slots, s32[8]{0:T(128)S(1)} %and_select_fusion.16.gslots, s32[8]{0:T(128)S(1)} %reshape.103.counts, bf16[8,64,256]{2,1,0:T(8,128)(2,1)S(1)} %bitcast.11, bf16[8,64,256]{2,1,0:T(8,128)(2,1)S(1)} %bitcast.8, bf16[8,64,256]{2,1,0:T(8,128)(2,1)S(1)} %bitcast.10, ...), custom_call_target="tpu_custom_call" | custom-call | tf_op jit(solution)/shard_map/attend/pallas_call | solution.py:382
  171.9 0.8 copy.24
  (8 shorter events, 0.1 us)
Async XLA Ops:
  4.1 1.0 copy-start.1
  5.0 0.9 copy-start.2
  149.3 1.2 copy-start
  150.5 0.9 copy-start.3

commit v3 on v2

v3 whole, which is shorter than its diff:
```python
import jax
import jax.numpy as jnp
from jax import lax
from jax.experimental import pallas as pl
from jax.experimental.pallas import tpu as pltpu
from jax.sharding import PartitionSpec as P

HEAD_DIM = 128
BLOCK = 64
GLOB = 2
RMAX = 4
NX, NZ, NC = 4, 16, 2
ROW = NX * NC
SEQS = 4
BPD = 2
OWN = SEQS * BPD
CAP = 16
PAIRS = 4
SPLIT = 4
PART = OWN // SPLIT
MESH = pl.DeviceIdType.MESH


GROUPS = ((0, 1), (1, 5), (5, 9), (9, 13), (13, 16))
ROWS = OWN * BLOCK
KEYS = (3 + GLOB + RMAX) * BLOCK
NY = 4
STEPS = ((5, 2), (6, 0), (6, 2), (7, 0))


def slot_of(d):
    return 0 if d == 0 else (2 * d - 1 if d < 8 else (15 if d == 8 else 2 * (NZ - d)))


ORDER = sorted(range(NZ), key=slot_of)


def exchange_kernel(
    q_any, k8, v8, k4, v4, w_any, req, gdist, gsel, gown, slots, counts, out, *scratch
):
    gath = [scratch[p * NZ : (p + 1) * NZ] for p in range(PAIRS)]
    rest = scratch[PAIRS * NZ :]
    cand_in, rcv, glob, win = (rest[i * PAIRS : (i + 1) * PAIRS] for i in range(4))
    (
        pack, cand, pick, req_in, req_s, q, w, weights, totals, att, att_in, partial,
        own_sem, z_send, z_recv, x_send, x_recv, c_send, c_recv, g_send, g_recv,
        h_send, h_recv, r_send, r_recv, s_sem, y_send, y_recv,
    ) = rest[4 * PAIRS :]
    ctx = lax.axis_index("ctx")
    head = lax.axis_index("head")
    x, z, c = ctx // (NZ * NC), (ctx // NC) % NZ, ctx % NC
    me = x * NC + c

    def at_z(step):
        return (x * (NZ * NC) + ((z + step + NZ) % NZ) * NC + c, head)

    def at_row(r):
        return ((r // NC) * (NZ * NC) + z * NC + r % NC, head)

    count = NX * NZ * NC
    right = ((ctx + 1) % count, head)
    left = ((ctx + count - 1) % count, head)

    own = [
        pltpu.make_async_copy(
            (k8, v8)[p % 2].at[:, :, pl.ds((p // 2) * HEAD_DIM, HEAD_DIM)],
            gath[p][0],
            own_sem.at[p],
        )
        for p in range(PAIRS)
    ]
    late = [
        pltpu.make_async_copy(
            (k4, v4)[p % 2].at[:, :, :, pl.ds((p // 2) * HEAD_DIM, HEAD_DIM)],
            win[p].at[:, pl.ds(1, BPD)],
            own_sem.at[PAIRS + p],
        )
        for p in range(PAIRS)
    ] + [
        pltpu.make_async_copy(q_any, q, own_sem.at[2 * PAIRS]),
        pltpu.make_async_copy(w_any, w, own_sem.at[2 * PAIRS + 1]),
    ]
    for copy in own:
        copy.start()
    own_req = pltpu.make_async_copy(req.at[0], req_s.at[0], s_sem.at[0])
    own_req.start()
    for copy in late:
        copy.start()

    barrier = pltpu.get_barrier_semaphore()
    peers = [at_z(1), at_z(-1), right, left] + [at_row((me + k) % ROW) for k in range(1, ROW)]
    peers += [(ctx, (head + k) % NY) for k in range(1, NY)]
    for peer in peers:
        pl.semaphore_signal(barrier, inc=1, device_id=peer, device_id_type=MESH)
    pl.semaphore_wait(barrier, len(peers))

    def req_copy(k):
        return pltpu.make_async_remote_copy(
            src_ref=req.at[k], dst_ref=req_in.at[k],
            send_sem=r_send.at[k], recv_sem=r_recv.at[k],
            device_id=at_row((me + ROW - k) % ROW), device_id_type=MESH,
        )

    for k in range(1, ROW):
        req_copy(k).start()

    def z_copy(p, way, t, a):
        if way == 0:
            src, dst, peer = (-t) % NZ, (-t - 1) % NZ, at_z(1)
        else:
            src, dst, peer = t, t + 1, at_z(-1)
        part = pl.ds(a * PART, PART)
        return pltpu.make_async_remote_copy(
            src_ref=gath[p][src].at[part],
            dst_ref=gath[p][dst].at[part],
            send_sem=z_send.at[p, (way * 8 + t) * SPLIT + a],
            recv_sem=z_recv.at[p, (way * 8 + t) * SPLIT + a],
            device_id=peer, device_id_type=MESH,
        )

    def used(way, t, a):
        return t < 7 or a // (SPLIT // 2) == way

    for copy in own:
        copy.wait()
    for a in range(SPLIT):
        for way in range(2):
            z_copy(0, way, 0, a).start()

    halos = [
        pltpu.make_async_remote_copy(
            src_ref=(k4, v4)[p % 2].at[:, 1 - side, :, pl.ds((p // 2) * HEAD_DIM, HEAD_DIM)],
            dst_ref=win[p].at[:, 3 * side],
            send_sem=h_send.at[2 * p + side],
            recv_sem=h_recv.at[2 * p + side],
            device_id=(right, left)[side], device_id_type=MESH,
        )
        for p in range(PAIRS)
        for side in range(2)
    ]
    for copy in halos:
        copy.start()

    own_req.wait()
    for k in range(1, ROW):
        req_copy(k).wait()
    lists = [
        pltpu.make_async_copy(req_in.at[k], req_s.at[k], s_sem.at[k]) for k in range(1, ROW)
    ]
    for copy in lists:
        copy.start()
    for copy in lists:
        copy.wait()

    def x_copy(p, g, k):
        low, high = GROUPS[g]
        return pltpu.make_async_remote_copy(
            src_ref=pack.at[p, k, pl.ds(low, high - low)],
            dst_ref=rcv[p].at[pl.ds(k * CAP + low, high - low)],
            send_sem=x_send.at[p * len(GROUPS) + g, k],
            recv_sem=x_recv.at[p * len(GROUPS) + g, k],
            device_id=at_row((me + k) % ROW), device_id_type=MESH,
        )

    def c_copy(p, k):
        return pltpu.make_async_remote_copy(
            src_ref=cand.at[p, (me + k) % ROW], dst_ref=cand_in[p].at[k],
            send_sem=c_send.at[p, k], recv_sem=c_recv.at[p, k],
            device_id=at_row((me + k) % ROW), device_id_type=MESH,
        )

    def g_copy(p, k):
        return pltpu.make_async_remote_copy(
            src_ref=pick.at[p], dst_ref=glob[p].at[k],
            send_sem=g_send.at[p, k], recv_sem=g_recv.at[p, k],
            device_id=at_row((me + k) % ROW), device_id_type=MESH,
        )

    def push(p, g):
        low, high = GROUPS[g]
        for n in range(low, high):
            rcv[p][n] = gath[p][ORDER[n]][req_s[0, 0, n]]

        def fill(k, carry):
            for n in range(low, high):
                pack[p, k, n] = gath[p][ORDER[n]][req_s[k, 0, n]]
            x_copy(p, g, k).start()
            return carry

        lax.fori_loop(1, ROW, fill, 0)

    def consider(p, dists):
        def one(q, carry):
            best = cand[p, q]
            for d in dists:
                best = lax.select(gdist[q] == d, gath[p][d][gsel[q]], best)
            cand[p, q] = best
            return carry

        lax.fori_loop(0, ROW, one, 0)

    def spread(p):
        def landed(k, carry):
            c_copy(p, k).wait_recv()
            return carry

        lax.fori_loop(1, ROW, landed, 0)
        chosen = cand_in[p][gown[0]]
        pick[p] = chosen
        glob[p][0] = chosen

        def send(k, carry):
            g_copy(p, k).start()
            return carry

        lax.fori_loop(1, ROW, send, 0)

    def settle(p):
        def landed(k, carry):
            g_copy(p, k).wait_recv()
            for g in range(len(GROUPS)):
                x_copy(p, g, k).wait_recv()
            return carry

        lax.fori_loop(1, ROW, landed, 0)
        for side in range(2):
            halos[2 * p + side].wait_recv()

    def rows(p, n):
        s, j = n // BPD, n % BPD
        window = [win[p][s, j + i] for i in range(3)]
        shared = [glob[p][(me + ROW - (s * GLOB + g)) % ROW] for g in range(GLOB)]
        picked = [rcv[p][slots[n * RMAX + r]] for r in range(RMAX)]
        return jnp.concatenate(window + shared + picked, axis=0)

    column = lax.broadcasted_iota(jnp.int32, (BLOCK, KEYS), 1)

    def score(h, low, high):
        def one(n, carry):
            live = column < (3 + GLOB) * BLOCK + counts[n] * BLOCK
            scores = lax.dot_general(
                q[n, :, h * HEAD_DIM : (h + 1) * HEAD_DIM], rows(2 * h, n),
                (((1,), (1,)), ((), ())), preferred_element_type=jnp.float32,
            ) * (HEAD_DIM ** (-0.5))
            masked = jnp.where(live, scores, -1e30)
            peak = jnp.max(masked, axis=-1, keepdims=True)
            grown = jnp.where(live, jnp.exp(masked - peak), 0.0)
            weights[n] = grown.astype(jnp.bfloat16)
            totals[n] = jnp.broadcast_to(
                jnp.sum(grown, axis=-1, keepdims=True), (BLOCK, HEAD_DIM)
            )
            return carry

        lax.fori_loop(low, high, one, 0)

    def mix(h, low, high):
        def one(n, carry):
            weighted = jnp.dot(
                weights[n], rows(2 * h + 1, n), preferred_element_type=jnp.float32
            )
            at = pl.ds(pl.multiple_of(n * BLOCK, BLOCK), BLOCK)
            att[h, at, :] = (weighted / totals[n]).astype(jnp.bfloat16)
            return carry

        lax.fori_loop(low, high, one, 0)

    def y_copy(k, h, part):
        at = pl.ds(part * (ROWS // 2), ROWS // 2)
        return pltpu.make_async_remote_copy(
            src_ref=att.at[h, at], dst_ref=att_in.at[k - 1, h, at],
            send_sem=y_send.at[k, 2 * h + part], recv_sem=y_recv.at[k, 2 * h + part],
            device_id=(ctx, (head + k) % NY), device_id_type=MESH,
        )

    def share(h, part):
        for k in range(1, NY):
            y_copy(k, h, part).start()

    def compute(p, step):
        h, quarter = p // 2, (2 * step, 2 * step + 2)
        if step == 0:
            settle(p)
        (mix if p % 2 else score)(h, *quarter)
        if p % 2 and step % 2:
            share(h, step // 2)

    def one_pair(p):
        def first(n, carry):
            cand[p, n] = gath[p][0][gsel[n]]
            return carry

        lax.fori_loop(0, ROW, first, 0)
        for t in range(1, 8):
            for a in range(SPLIT):
                for way in range(2):
                    z_copy(p, way, t - 1, a).wait_recv()
                    if used(way, t, a):
                        z_copy(p, way, t, a).start()
                    if t == 7 and p < PAIRS - 1:
                        z_copy(p + 1, way, 0, a).start()
                if p > 0 and (t, a) in STEPS:
                    compute(p - 1, STEPS.index((t, a)))
            consider(p, (t, NZ - t))
            if t % 2 == 0:
                push(p, t // 2)
            if t == 3 and p > 0:
                spread(p - 1)
        for a in range(SPLIT):
            z_copy(p, a // (SPLIT // 2), 7, a).wait_recv()
        consider(p, (8,))

        def offer(k, carry):
            c_copy(p, k).start()
            return carry

        lax.fori_loop(1, ROW, offer, 0)
        push(p, 4)
        cand_in[p][0] = cand[p, me]

    for p in range(PAIRS):
        push(p, 0)
    for copy in late:
        copy.wait()
    for p in range(PAIRS):
        one_pair(p)
    spread(PAIRS - 1)
    for step in range(4):
        compute(PAIRS - 1, step)

    def feature_rows(k, h):
        start = ((head + NY - k) % NY) * (2 * HEAD_DIM) + h * HEAD_DIM
        return w[pl.ds(pl.multiple_of(start, HEAD_DIM), HEAD_DIM), :]

    for k in range(1, NY):
        for part in range(2):
            y_copy(k, 0, part).wait_recv()

    def project_first(i, carry):
        at = pl.ds(pl.multiple_of(i * 128, 128), 128)
        total = jnp.dot(att[0, at, :], feature_rows(0, 0), preferred_element_type=jnp.float32)
        total += jnp.dot(att[1, at, :], feature_rows(0, 1), preferred_element_type=jnp.float32)
        for k in range(1, NY):
            total += jnp.dot(
                att_in[k - 1, 0, at, :], feature_rows(k, 0), preferred_element_type=jnp.float32
            )
        partial[at, :] = total
        return carry

    lax.fori_loop(0, ROWS // 128, project_first, 0)
    for k in range(1, NY):
        for part in range(2):
            y_copy(k, 1, part).wait_recv()

    def project_last(i, carry):
        at = pl.ds(pl.multiple_of(i * 128, 128), 128)
        total = partial[at, :]
        for k in range(1, NY):
            total += jnp.dot(
                att_in[k - 1, 1, at, :], feature_rows(k, 1), preferred_element_type=jnp.float32
            )
        out[at, :] = total.astype(jnp.bfloat16)
        return carry

    lax.fori_loop(0, ROWS // 128, project_last, 0)

    for copy in halos:
        copy.wait_send()
    for k in range(1, NY):
        for h in range(2):
            for part in range(2):
                y_copy(k, h, part).wait_send()
    for p in range(PAIRS):
        for way in range(2):
            for t in range(8):
                for a in range(SPLIT):
                    if used(way, t, a):
                        z_copy(p, way, t, a).wait_send()

        def ends(k, carry, p=p):
            c_copy(p, k).wait_send()
            g_copy(p, k).wait_send()
            for g in range(len(GROUPS)):
                x_copy(p, g, k).wait_send()
            return carry

        lax.fori_loop(1, ROW, ends, 0)


def exchange(q, keys, values, w, req, gdist, gsel, gown, slots, counts):
    width = q.shape[-1]
    block = (BLOCK, HEAD_DIM)
    dma = pltpu.SemaphoreType.DMA
    bf16 = jnp.bfloat16
    hbm = pl.BlockSpec(memory_space=pl.ANY)
    vmem = pl.BlockSpec(memory_space=pltpu.VMEM)
    smem = pl.BlockSpec(memory_space=pltpu.SMEM)
    k8, v8 = (kv.reshape(OWN, BLOCK, width) for kv in (keys, values))
    k4, v4 = (kv.reshape(SEQS, BPD, BLOCK, width) for kv in (keys, values))
    return pl.pallas_call(
        exchange_kernel,
        out_shape=jax.ShapeDtypeStruct((ROWS, w.shape[1]), bf16),
        in_specs=[hbm] * 6 + [vmem] + [smem] * 5,
        out_specs=vmem,
        scratch_shapes=[
            *([pltpu.VMEM((OWN,) + block, bf16)] * (PAIRS * NZ)),
            *([pltpu.VMEM((ROW,) + block, bf16)] * PAIRS),
            *([pltpu.VMEM((ROW * CAP,) + block, bf16)] * PAIRS),
            *([pltpu.VMEM((ROW,) + block, bf16)] * PAIRS),
            *([pltpu.VMEM((SEQS, BPD + 2) + block, bf16)] * PAIRS),
            pltpu.VMEM((PAIRS, ROW, CAP) + block, bf16),
            pltpu.VMEM((PAIRS, ROW) + block, bf16),
            pltpu.VMEM((PAIRS,) + block, bf16),
            pltpu.VMEM((ROW, 8, 128), jnp.int32),
            pltpu.SMEM((ROW, 8, 128), jnp.int32),
            pltpu.VMEM((OWN, BLOCK, width), bf16),
            pltpu.VMEM(w.shape, bf16),
            pltpu.VMEM((OWN, BLOCK, KEYS), bf16),
            pltpu.VMEM((OWN,) + block, jnp.float32),
            pltpu.VMEM((2, ROWS, HEAD_DIM), bf16),
            pltpu.VMEM((NY - 1, 2, ROWS, HEAD_DIM), bf16),
            pltpu.VMEM((ROWS, w.shape[1]), jnp.float32),
            dma((2 * PAIRS + 2,)),
            dma((PAIRS, 16 * SPLIT)), dma((PAIRS, 16 * SPLIT)),
            dma((PAIRS * len(GROUPS), ROW)), dma((PAIRS * len(GROUPS), ROW)),
            dma((PAIRS, ROW)), dma((PAIRS, ROW)),
            dma((PAIRS, ROW)), dma((PAIRS, ROW)),
            dma((2 * PAIRS,)), dma((2 * PAIRS,)),
            dma((ROW,)), dma((ROW,)),
            dma((ROW,)),
            dma((NY, 4)), dma((NY, 4)),
        ],
        compiler_params=pltpu.CompilerParams(
            collective_id=0, has_side_effects=True, vmem_limit_bytes=52 << 20
        ),
        name="exchange",
    )(q, k8, v8, k4, v4, w, req, gdist, gsel, gown, slots, counts)


def on_device(queries, keys, values, out_weight, global_ids, rand_ids, rand_count):
    seq_count, seq_rows, width = queries.shape
    q = queries.reshape(OWN, BLOCK, width)
    ctx = lax.axis_index("ctx")
    my_z = (ctx // NC) % NZ
    me = (ctx // (NZ * NC)) * NC + ctx % NC

    def place(ids, seq):
        owner = ids // BPD
        row = (owner // (NZ * NC)) * NC + owner % NC
        dist = ((owner // NC) % NZ - my_z) % NZ
        return row, dist, seq * BPD + ids % BPD

    seq_of = jnp.arange(SEQS, dtype=jnp.int32)
    row, dist, choice = place(rand_ids, seq_of[:, None, None])
    live = (jnp.arange(RMAX, dtype=jnp.int32) < rand_count[:, :, None]).reshape(-1)
    where = jnp.where(dist < 8, jnp.maximum(2 * dist - 1, 0), 2 * (NZ - dist))
    where = jnp.where(dist == 8, CAP - 1, where)
    slots = jnp.where(live, (((me - row) % ROW) * CAP + where).reshape(-1), 0)
    lane = jnp.arange(128, dtype=jnp.int32)
    place_of = jnp.arange(ROW, dtype=jnp.int32)[:, None] * CAP + lane
    hit = (place_of[:, :, None] == slots) & live & (lane < CAP)[None, :, None]
    req = jnp.max(jnp.where(hit, choice.reshape(-1), 0), axis=2)
    req = jnp.broadcast_to(req[:, None, :], (ROW, 8, 128))

    grow, gdist, gsel = place(global_ids, seq_of[:, None])
    gown = ((me - grow.reshape(-1)) % ROW)[me].reshape(1)

    return exchange(
        q, keys, values, out_weight, req, gdist.reshape(-1), gsel.reshape(-1), gown,
        slots, rand_count.reshape(-1),
    ).reshape(seq_count, seq_rows, out_weight.shape[1])


def solution(mesh):
    placed = (
        P(None, "ctx", "head"),
        P(None, "ctx", "head"),
        P(None, "ctx", "head"),
        P(None, "head"),
        P(),
        P(None, "ctx", None),
        P(None, "ctx"),
    )
    return jax.shard_map(
        on_device, mesh=mesh, in_specs=placed, out_specs=P(None, "ctx", "head"), check_vma=False
    )
```

time: 173 us -> 166 us (0.960)
  Pallas kernels: 164 us -> 158 us
    pallas_call x2 -> x1, Pallas kernels: 164 us -> 158 us  [exchange(): pl.pallas_call(exchange_kernel, out_shape=jax.ShapeDtypeStruct((ROWS, w.s...]
    unnamed x10 -> x14, local copies, waits for them, and re-layouts: 5.63 us -> 5.52 us
where the time goes in v3:
time: 166 us
  Pallas kernels  158 us (95%)
  local copies, waits for them, and re-layouts  6.99 us (4%)
    pallas_call x1, Pallas kernels, exchange(): pl.pallas_call(exchange_kernel, out_shape=jax.ShapeDtypeStruct((ROWS, w.s...  158 us
    unnamed x14, local copies, waits for them, and re-layouts  5.52 us

profile of v3, /device:TPU:1, one launch (start us, length us, event | category | flops | bytes accessed | tf_op | source)
XLA Modules:
  0.0 165.5 jit_solution(5927256176557269600)
XLA Ops:
  0.0 0.0 copy-start.4
  0.0 0.7 copy-done.4
  0.7 0.1 copy.18
  0.8 0.1 reshape.114.counts
  0.9 0.1 iota_compare_fusion
  0.9 0.0 copy-start.5
  0.9 0.1 lt.99
  1.0 0.6 copy-done.5
  1.6 0.1 copy.21
  1.7 0.1 sub.83
  1.8 0.6 dynamic_slice.3.gown
  2.4 0.1 copy.19
  2.5 0.1 reshape.112.gdist
  2.6 0.1 copy.20
  2.7 0.0 copy-start.3
  2.7 0.1 reshape.113.gsel
  2.8 0.1 iota_add_fusion
  2.9 0.5 copy-done.3
  3.4 0.1 fusion.2
  3.5 0.1 reshape.110
  3.6 0.1 reshape.111
  3.7 0.1 select_reduce_fusion
  3.8 0.0 copy-start
  3.8 0.9 copy-done
  4.8 0.0 copy-start.1
  4.8 0.9 copy-done.1
  5.7 0.0 copy-start.2
  5.7 0.9 copy-done.2
  6.7 158.1 %exchange.1 = bf16[512,512]{1,0:T(8,128)(2,1)S(1)} custom-call(bf16[8,64,256]{2,1,0:T(8,128)(2,1)S(1)} %bitcast.11, bf16[8,64,256]{2,1,0:T(8,128)(2,1)S(1)} %bitcast.7, bf16[8,64,256]{2,1,0:T(8,128)(2,1)S(1)} %bitcast.9, bf16[4,2,64,256]{3,2,1,0:T(8,128)(2,1)S(1)} %bitcast.8, bf16[4,2,64,256]{3,2,1,0:T(8,128)(2,1)S(1)} %bitcast.10, bf16[1024,512]{1,0:T(8,128)(2,1)} %w_any.1, ...), custom_call_target="tpu_custom_call" | custom-call | tf_op jit(solution)/shard_map/exchange/pallas_call | solution.py:399
  164.7 0.8 copy.24
  (8 shorter events, 0.1 us)
Async XLA Ops:
  0.0 0.7 copy-start.4
  0.9 0.7 copy-start.5
  2.7 0.7 copy-start.3
  3.8 1.0 copy-start
  4.8 0.9 copy-start.1
  5.7 0.9 copy-start.2

commit v4 on v3

--- a/solution.py
+++ b/solution.py
@@ -16,16 +16,15 @@
 OWN = SEQS * BPD
 CAP = 16
 PAIRS = 4
-SPLIT = 4
+SPLIT = 2
 PART = OWN // SPLIT
 MESH = pl.DeviceIdType.MESH
 
 
-GROUPS = ((0, 1), (1, 5), (5, 9), (9, 13), (13, 16))
+GROUPS = ((0, 1), (1, 3), (3, 7), (7, 11), (11, 15), (15, 16))
 ROWS = OWN * BLOCK
 KEYS = (3 + GLOB + RMAX) * BLOCK
 NY = 4
-STEPS = ((5, 2), (6, 0), (6, 2), (7, 0))
 
 
 def slot_of(d):
@@ -124,8 +123,9 @@
     for copy in own:
         copy.wait()
     for a in range(SPLIT):
-        for way in range(2):
-            z_copy(0, way, 0, a).start()
+        for p in range(2):
+            for way in range(2):
+                z_copy(p, way, 0, a).start()
 
     halos = [
         pltpu.make_async_remote_copy(
@@ -276,56 +276,64 @@
         for k in range(1, NY):
             y_copy(k, h, part).start()
 
-    def compute(p, step):
-        h, quarter = p // 2, (2 * step, 2 * step + 2)
-        if step == 0:
-            settle(p)
-        (mix if p % 2 else score)(h, *quarter)
-        if p % 2 and step % 2:
-            share(h, step // 2)
-
-    def one_pair(p):
+    def compute(h, step):
+        low = 2 * (step % 4)
+        if step % 4 == 0:
+            settle(2 * h + step // 4)
+        (score, mix)[step // 4](h, low, low + 2)
+        if step > 4 and step % 2:
+            share(h, (step - 4) // 2)
+
+    def one_head(h):
+        both = (2 * h, 2 * h + 1)
+
         def first(n, carry):
-            cand[p, n] = gath[p][0][gsel[n]]
+            for p in both:
+                cand[p, n] = gath[p][0][gsel[n]]
             return carry
 
         lax.fori_loop(0, ROW, first, 0)
         for t in range(1, 8):
             for a in range(SPLIT):
-                for way in range(2):
-                    z_copy(p, way, t - 1, a).wait_recv()
-                    if used(way, t, a):
-                        z_copy(p, way, t, a).start()
-                    if t == 7 and p < PAIRS - 1:
-                        z_copy(p + 1, way, 0, a).start()
-                if p > 0 and (t, a) in STEPS:
-                    compute(p - 1, STEPS.index((t, a)))
-            consider(p, (t, NZ - t))
-            if t % 2 == 0:
-                push(p, t // 2)
-            if t == 3 and p > 0:
-                spread(p - 1)
-        for a in range(SPLIT):
-            z_copy(p, a // (SPLIT // 2), 7, a).wait_recv()
-        consider(p, (8,))
-
-        def offer(k, carry):
-            c_copy(p, k).start()
-            return carry
-
-        lax.fori_loop(1, ROW, offer, 0)
-        push(p, 4)
-        cand_in[p][0] = cand[p, me]
+                for p in both:
+                    for way in range(2):
+                        z_copy(p, way, t - 1, a).wait_recv()
+                        if used(way, t, a):
+                            z_copy(p, way, t, a).start()
+                        if t == 7 and h == 0:
+                            z_copy(p + 2, way, 0, a).start()
+                if h > 0 and t >= 4:
+                    compute(h - 1, 2 * (t - 4) + a)
+            for p in both:
+                consider(p, (t, NZ - t))
+                if t % 2:
+                    push(p, (t + 1) // 2)
+                if t == 3 and h > 0:
+                    spread(p - 2)
+        for p in both:
+            for a in range(SPLIT):
+                z_copy(p, a // (SPLIT // 2), 7, a).wait_recv()
+            consider(p, (8,))
+
+            def offer(k, carry, p=p):
+                c_copy(p, k).start()
+                return carry
+
+            lax.fori_loop(1, ROW, offer, 0)
+            cand_in[p][0] = cand[p, me]
+        for p in both:
+            push(p, 5)
 
     for p in range(PAIRS):
         push(p, 0)
     for copy in late:
         copy.wait()
-    for p in range(PAIRS):
-        one_pair(p)
-    spread(PAIRS - 1)
-    for step in range(4):
-        compute(PAIRS - 1, step)
+    for h in range(2):
+        one_head(h)
+    for p in (2, 3):
+        spread(p)
+    for step in range(8):
+        compute(1, step)
 
     def feature_rows(k, h):
         start = ((head + NY - k) % NY) * (2 * HEAD_DIM) + h * HEAD_DIM

time: 166 us -> 160 us (0.964)
  Pallas kernels: 158 us -> 153 us
    pallas_call x1, Pallas kernels: 158 us -> 153 us  [exchange(): pl.pallas_call(exchange_kernel, out_shape=jax.ShapeDtypeStruct((ROWS, w.s...]
where the time goes in v4:
time: 160 us
  Pallas kernels  153 us (96%)
  local copies, waits for them, and re-layouts  6.99 us (4%)
    pallas_call x1, Pallas kernels, exchange(): pl.pallas_call(exchange_kernel, out_shape=jax.ShapeDtypeStruct((ROWS, w.s...  153 us
    unnamed x14, local copies, waits for them, and re-layouts  5.52 us

profile of v4, /device:TPU:1, one launch (start us, length us, event | category | flops | bytes accessed | tf_op | source)
XLA Modules:
  0.0 160.0 jit_solution(5806058691090834601)
XLA Ops:
  0.0 0.0 copy-start.4
  0.0 0.7 copy-done.4
  0.7 0.1 copy.18
  0.8 0.1 reshape.114.counts
  0.9 0.1 iota_compare_fusion
  0.9 0.0 copy-start.5
  0.9 0.1 lt.99
  1.0 0.6 copy-done.5
  1.6 0.1 copy.21
  1.7 0.1 sub.83
  1.8 0.6 dynamic_slice.3.gown
  2.4 0.1 copy.19
  2.5 0.1 reshape.112.gdist
  2.6 0.1 copy.20
  2.7 0.0 copy-start.3
  2.7 0.1 reshape.113.gsel
  2.8 0.1 iota_add_fusion
  2.9 0.5 copy-done.3
  3.4 0.1 fusion.2
  3.5 0.1 reshape.110
  3.6 0.1 reshape.111
  3.7 0.1 select_reduce_fusion
  3.8 0.0 copy-start
  3.8 0.9 copy-done
  4.8 0.0 copy-start.1
  4.8 0.9 copy-done.1
  5.7 0.0 copy-start.2
  5.7 0.9 copy-done.2
  6.7 152.5 %exchange.1 = bf16[512,512]{1,0:T(8,128)(2,1)S(1)} custom-call(bf16[8,64,256]{2,1,0:T(8,128)(2,1)S(1)} %bitcast.11, bf16[8,64,256]{2,1,0:T(8,128)(2,1)S(1)} %bitcast.7, bf16[8,64,256]{2,1,0:T(8,128)(2,1)S(1)} %bitcast.9, bf16[4,2,64,256]{3,2,1,0:T(8,128)(2,1)S(1)} %bitcast.8, bf16[4,2,64,256]{3,2,1,0:T(8,128)(2,1)S(1)} %bitcast.10, bf16[1024,512]{1,0:T(8,128)(2,1)} %w_any.1, ...), custom_call_target="tpu_custom_call" | custom-call | tf_op jit(solution)/shard_map/exchange/pallas_call | solution.py:407
  159.2 0.8 copy.24
  (8 shorter events, 0.1 us)
Async XLA Ops:
  0.0 0.7 copy-start.4
  0.9 0.7 copy-start.5
  2.7 0.7 copy-start.3
  3.8 1.0 copy-start
  4.8 0.9 copy-start.1
  5.7 0.9 copy-start.2
